TPU v7x, 32 devices: a whole 2x2x4 slice. The times are simulated.
32 devices in a mesh: groups: 2 (over x), depth: 8 (over z, y), height: 2 (over core).
Axes of the slice: x: 2, y: 2, z: 4, core: 2. Of those that a mesh axis runs over, the one named last changes fastest.
Arguments:
- images: bfloat16 [4, 4, 64, 16, 256], P('groups', None, 'depth', 'height'), parts along dimension 0, may hold values from -6 to 6
- pre_hidden: bfloat16 [4, 16, 64, 16, 256], P('groups', None, 'depth', 'height'), parts along dimension 0, may hold values from -6 to 6
- pre_deep: bfloat16 [4, 32, 32, 8, 128], P(('groups', 'height'), None, 'depth'), parts along dimension 0, may hold values from -6 to 6
- pooled_grad: bfloat16 [4, 32, 16, 256], P(('groups', 'height'), None, 'depth'), parts along dimension 0, may hold values from -1.25 to 1.25
- deep_weight: bfloat16 [32, 16, 3, 3, 3], replicated, may hold values from -0.3125 to 0.3125
Outputs:
- first_kernel: float32 [32, 4, 3, 3, 3], P('groups'), parts along dimension 0
- first_bias: float32 [32], P('groups'), parts along dimension 0
- deep_kernel: float32 [64, 16, 3, 3, 3], P('groups'), parts along dimension 0
- deep_bias: float32 [64], P('groups'), parts along dimension 0
There are 2 independent parts, one for each index of `groups`. A program takes and returns all parts, laid end to end along the dimension named above; an argument that names none is the same for every part. Nothing has to cross between parts.
All inputs are finite; a program needn't handle non-finite values.
Results may differ from a plain program's by a relative error of at most 0.0031.
Values may be sent and summed in bfloat16 or wider, within the bound.
A program may use at most 128 MiB of HBM per device.

v0:
```python
import jax
import jax.numpy as jnp
from jax import lax
from jax.sharding import PartitionSpec as P

SLOPE = 0.3


def padded_2(block, sides, width):
    for axis, dim in sides:
        count = lax.axis_size(axis)
        forward = [(i, i + 1) for i in range(count - 1)]
        backward = [(target, source) for source, target in forward]
        low = lax.ppermute(
            lax.slice_in_dim(block, block.shape[dim] - width, None, axis=dim), axis, forward
        )
        high = lax.ppermute(lax.slice_in_dim(block, 0, width, axis=dim), axis, backward)
        block = jnp.concatenate([low, block, high], axis=dim)
    return block


def from_behind(value, axis, steps):
    count = lax.axis_size(axis)
    leading, last = (max(0, -steps), min(count, count - steps))
    return lax.ppermute(value, axis, [(source, source + steps) for source in range(leading, last)])


def leaky(values):
    return jnp.where(values > 0, values, SLOPE * values)


def slope_at(values):
    return jnp.where(values > 0, 1.0, SLOPE)


def deep_gradient(pooled_grad, pre_deep):
    samples, chans, quarter, flat = pooled_grad.shape
    half_depth, half_height, half_width = (pre_deep.shape[2], pre_deep.shape[3], pre_deep.shape[4])
    coarse = (
        pooled_grad.astype(jnp.float32).reshape(
            samples, chans, quarter, 1, half_height // 2, 1, half_width // 2, 1
        )
        / 8.0
    )
    spread = jnp.broadcast_to(
        coarse, (samples, chans, quarter, 2, half_height // 2, 2, half_width // 2, 2)
    )
    spread = spread.reshape(samples, chans, half_depth, half_height, half_width)
    return (spread * slope_at(pre_deep.astype(jnp.float32))).astype(jnp.bfloat16)


def deep_weight_grad(local_grad, padded):
    samples, chans = (padded.shape[0], padded.shape[1])
    coarse_depth, coarse_height, coarse_width = (
        local_grad.shape[2],
        local_grad.shape[3],
        local_grad.shape[4],
    )
    grown = jnp.pad(padded, ((0, 0), (0, 0), (0, 1), (0, 1), (0, 1)))
    phases = grown.reshape(
        samples, chans, coarse_depth + 1, 2, coarse_height + 1, 2, coarse_width + 1, 2
    )
    phases = phases.transpose(0, 1, 3, 5, 7, 2, 4, 6)
    kernels = []
    for depth_tap in range(3):
        for height_tap in range(3):
            for width_tap in range(3):
                depth_off, height_off, width_off = (depth_tap // 2, height_tap // 2, width_tap // 2)
                view = phases[
                    :,
                    :,
                    depth_tap % 2,
                    height_tap % 2,
                    width_tap % 2,
                    depth_off : depth_off + coarse_depth,
                    height_off : height_off + coarse_height,
                    width_off : width_off + coarse_width,
                ]
                kernels.append(
                    jnp.einsum(
                        "sodhw,sidhw->oi", local_grad, view, preferred_element_type=jnp.float32
                    )
                )
    kernel = jnp.stack(kernels, axis=-1).reshape(local_grad.shape[1], chans, 3, 3, 3)
    return (kernel, jnp.sum(local_grad, axis=(0, 2, 3, 4), dtype=jnp.float32))


def transpose_conv(extended, deep_weight):
    samples = extended.shape[0]
    coarse_depth, coarse_height, coarse_width = (
        extended.shape[2] - 1,
        extended.shape[3] - 1,
        extended.shape[4] - 1,
    )
    out_chans = deep_weight.shape[1]
    phase_taps = (((1, 0),), ((2, 0), (0, 1)))
    phases = []
    for depth_phase in range(2):
        for height_phase in range(2):
            for width_phase in range(2):
                views = []
                mats = []
                for depth_tap, depth_step in phase_taps[depth_phase]:
                    for height_tap, height_step in phase_taps[height_phase]:
                        for width_tap, width_step in phase_taps[width_phase]:
                            views.append(
                                extended[
                                    :,
                                    :,
                                    depth_step : depth_step + coarse_depth,
                                    height_step : height_step + coarse_height,
                                    width_step : width_step + coarse_width,
                                ]
                            )
                            mats.append(deep_weight[:, :, depth_tap, height_tap, width_tap])
                stacked = jnp.concatenate(views, axis=1)
                matrix = jnp.concatenate(mats, axis=0)
                phases.append(
                    jnp.einsum(
                        "sodhw,oi->sidhw", stacked, matrix, preferred_element_type=jnp.float32
                    )
                )
    grid = jnp.stack(phases, axis=0).reshape(
        2, 2, 2, samples, out_chans, coarse_depth, coarse_height, coarse_width
    )
    woven = grid.transpose(3, 4, 5, 0, 6, 1, 7, 2).reshape(
        samples, out_chans, 2 * coarse_depth, 2 * coarse_height, 2 * coarse_width
    )
    return woven.astype(jnp.bfloat16)


def first_weight_grad(first_grad, framed):
    chans = framed.shape[1]
    cells_depth, cells_height, cells_width = (
        first_grad.shape[2],
        first_grad.shape[3],
        first_grad.shape[4],
    )
    kernels = []
    for depth_tap in range(3):
        for height_tap in range(3):
            for width_tap in range(3):
                view = framed[
                    :,
                    :,
                    depth_tap : depth_tap + cells_depth,
                    height_tap : height_tap + cells_height,
                    width_tap : width_tap + cells_width,
                ]
                kernels.append(
                    jnp.einsum(
                        "sodhw,sidhw->oi", first_grad, view, preferred_element_type=jnp.float32
                    )
                )
    kernel = jnp.stack(kernels, axis=-1).reshape(first_grad.shape[1], chans, 3, 3, 3)
    return (kernel, jnp.sum(first_grad, axis=(0, 2, 3, 4), dtype=jnp.float32))


def on_device(images, pre_hidden, pre_deep, pooled_grad, deep_weight):
    deep_grad = deep_gradient(pooled_grad, pre_deep)
    hidden = leaky(pre_hidden.astype(jnp.float32)).astype(jnp.bfloat16)
    bordered = padded_2(images, (("depth", 2), ("height", 3)), 1)
    framed = jnp.pad(bordered, ((0, 0), (0, 0), (0, 0), (0, 0), (1, 1)))
    gathered = lax.all_to_all(hidden, "height", split_axis=0, concat_axis=3, tiled=True)
    below = from_behind(gathered[:, :, -1:], "depth", 1)
    padded = jnp.pad(
        jnp.concatenate([below, gathered], axis=2), ((0, 0), (0, 0), (0, 0), (1, 0), (1, 0))
    )
    above = from_behind(deep_grad[:, :, :1], "depth", -1)
    extended = jnp.pad(
        jnp.concatenate([deep_grad, above], axis=2), ((0, 0), (0, 0), (0, 0), (0, 1), (0, 1))
    )
    returned = transpose_conv(extended, deep_weight)
    hidden_grad = lax.all_to_all(returned, "height", split_axis=3, concat_axis=0, tiled=True)
    deep_kernel, deep_bias = deep_weight_grad(deep_grad, padded)
    first_grad = (
        hidden_grad.astype(jnp.float32) * slope_at(pre_hidden.astype(jnp.float32))
    ).astype(jnp.bfloat16)
    first_kernel, first_bias = first_weight_grad(first_grad, framed)
    first_kernel, first_bias, deep_kernel, deep_bias = lax.psum(
        (first_kernel, first_bias, deep_kernel, deep_bias), ("depth", "height")
    )
    return (first_kernel, first_bias, deep_kernel, deep_bias)


def solution(mesh):
    return jax.shard_map(
        on_device,
        mesh=mesh,
        in_specs=(
            P("groups", None, "depth", "height", None),
            P("groups", None, "depth", "height", None),
            P(("groups", "height"), None, "depth", None, None),
            P(("groups", "height"), None, "depth", None),
            P(),
        ),
        out_specs=(
            P("groups", None, None, None, None),
            P("groups"),
            P("groups", None, None, None, None),
            P("groups"),
        ),
        check_vma=False,
    )
```

profile of v0, /device:TPU:0, one launch (start us, length us, event | category | flops | bytes accessed | tf_op | source)
XLA Modules:
  0.0 230.6 jit_solution(8759666628445355263)
XLA Ops:
  0.6 1.2 copy.92
  2.5 1.3 collective-permute-start.2
  3.8 6.1 %collective-permute-start.1 = (bf16[2,4,1,8,256]{4,1,0,3,2:T(4,128)(2,1)}, bf16[2,4,1,8,256]{4,1,0,3,2:T(4,128)(2,1)}, u32[]{:S(2)}, u32[]{:S(2)}) collective-permute-start(bf16[2,4,1,8,256]{4,1,0,3,2:T(4,128)(2,1)} %get-tuple-element.24), channel_id=1, source_target_pairs={{0,2},{2,4},{4,6},{6,8},{8,10},{10,12},{12,14},{1,3},{3,5},{5,7},{... | collective-permute-start | bytes 98312 | tf_op jit(solution)/shard_map/ppermute | solution.py:14
  10.9 0.9 broadcast_in_dim.23
  13.2 1.3 collective-permute-start
  18.3 1.2 constant_dynamic-update-slice_fusion.8
  21.0 2.1 collective-permute-start.3
  23.0 1.3 collective-permute-start.4
  28.2 14.3 %copy.88 = bf16[2,2,2,1,16,4,8,128]{4,2,7,1,6,0,5,3:T(2,128)(2,1)} copy(bf16[2,2,2,1,16,4,8,128]{7,4,6,5,2,1,0,3:T(8,128)(2,1)S(1)} %bitcast.783) | data formatting | bytes 2097152 | tf_op jit(solution)/shard_map/convert_element_type | solution.py:129
  42.5 6.9 %copy.89 = bf16[1,16,8,16,256]{4,2,1,0,3:T(8,128)(2,1)S(1)} copy(bf16[1,16,8,16,256]{1,4,3,2,0:T(8,128)(2,1)} %bitcast.752) | data formatting | bytes 2097152 | tf_op jit(solution)/shard_map/convert_element_type | solution.py:129
  49.4 5.9 %all_to_all.27 = bf16[1,16,8,16,256]{4,2,1,0,3:T(8,128)(2,1)S(1)} all-to-all(bf16[1,16,8,16,256]{4,2,1,0,3:T(8,128)(2,1)S(1)} %copy.89), channel_id=1, replica_groups=mesh['groups'=2,'depth'=8,'height'=2] {'height'}, dimensions={3} | all-to-all | bytes 2097152 | tf_op jit(solution)/shard_map/all_to_all | solution.py:174
  55.3 1.3 convert_reduce_fusion
  56.8 4.7 %all_to_all.28 = bf16[2,16,8,8,256]{4,3,2,1,0:T(8,128)(2,1)S(1)} all-to-all(bf16[2,16,8,8,256]{4,3,2,1,0:T(8,128)(2,1)S(1)} %copy.125), channel_id=1, replica_groups=mesh['groups'=2,'depth'=8,'height'=2] {'height'}, dimensions={0} | all-to-all | bytes 2097152 | tf_op jit(solution)/shard_map/all_to_all | solution.py:164
  61.6 4.9 %collective-permute-start.5 = (bf16[1,16,1,16,256]{4,3,2,1,0:T(8,128)(2,1)S(1)}, bf16[1,16,1,16,256]{4,3,2,1,0:T(8,128)(2,1)S(1)}, u32[]{:S(2)}, u32[]{:S(2)}) collective-permute-start(bf16[1,16,1,16,256]{4,3,2,1,0:T(8,128)(2,1)S(1)} %slice.448), channel_id=1, source_target_pairs={{0,2},{2,4},{4,6},{6,8},{8,10},{10,12},{12,14},{1,3},{3,5},{5,7},{... | collective-permute-start | bytes 393224 | tf_op jit(solution)/shard_map/ppermute | solution.py:25
  66.5 1.4 select_maximum_fusion
  68.7 1.6 fusion.81
  70.3 0.9 fusion.80
  72.0 1.6 fusion.78
  75.2 1.6 fusion.75
  76.8 0.9 fusion.74
  78.5 1.6 fusion.72
  80.1 0.9 fusion.71
  81.8 0.9 fusion.69
  84.4 1.8 fusion.66
  87.9 1.6 fusion.63
  91.1 1.6 fusion.60
  94.4 1.6 fusion.57
  97.0 6.6 %copy.193 = bf16[1,16,9,16,256]{1,4,3,2,0:T(8,128)(2,1)} copy(bf16[1,16,9,16,256]{4,3,2,1,0:T(8,128)(2,1)S(1)} %pad_maximum_fusion.4) | data formatting | bytes 2359296
  103.6 10.9 %pad.82 = bf16[1,16,10,18,258]{1,4,3,2,0:T(8,128)(2,1)} pad(bf16[1,16,9,16,256]{1,4,3,2,0:T(8,128)(2,1)} %copy.193, bf16[]{:T(256)} %constant.3.clone.1), padding=0_0x0_0x0_1x1_1x1_1 | pad | bytes 2665730 | tf_op jit(solution)/shard_map/jit(_pad)/pad | solution.py:59
  114.5 24.0 %reshape.237 = bf16[1,16,5,2,9,2,129,2]{1,7,6,5,4,3,2,0:T(2,128)(2,1)} reshape(bf16[1,16,10,18,258]{1,4,3,2,0:T(8,128)(2,1)} %pad.82) | data formatting | bytes 2972160 | tf_op jit(solution)/shard_map/reshape | solution.py:60
  138.5 22.6 %copy.128 = bf16[1,16,5,2,9,2,129,2]{6,1,4,2,7,5,3,0:T(8,128)(2,1)S(1)} copy(bf16[1,16,5,2,9,2,129,2]{1,7,6,5,4,3,2,0:T(2,128)(2,1)} %reshape.237) | data formatting | bytes 2972160 | tf_op jit(solution)/shard_map/reshape | solution.py:60
  166.9 63.7 %all-reduce.4 = (f32[16,4,3,3,3]{0,1,4,3,2:T(4,128)}, f32[16]{0:T(128)}, f32[32,16,3,3,3]{0,1,4,3,2:T(8,128)}, f32[32]{0:T(128)}) all-reduce(f32[16,4,3,3,3]{0,1,4,3,2:T(4,128)S(1)} %bitcast.786, f32[16]{0:T(128)S(1)} %get-tuple-element.10, ...), channel_id=1, replica_groups=mesh['groups'=2,'depth'=8,'height'=2] {'depth','height'}, use_global_device_ids=true, to_apply=%region_0.1 | all-reduce | flops 15600 | bytes 124800 | tf_op jit(solution)/shard_map/psum | solution.py:180
  (135 shorter events, 30.4 us)
Async XLA Ops:
  1.8 8.1 %copy-start.4 = (bf16[2,4,8,8,256]{4,1,0,3,2:T(4,128)(2,1)}, bf16[2,4,8,8,256]{4,1,0,3,2:T(4,128)(2,1)S(1)}, u32[]{:S(2)}) copy-start(bf16[2,4,8,8,256]{4,1,0,3,2:T(4,128)(2,1)S(1)} %copy.92) | copy-start | bytes 786436
  2.5 16.9 %collective-permute-start.2 = (bf16[2,4,1,8,256]{4,1,0,3,2:T(4,128)(2,1)}, bf16[2,4,1,8,256]{4,1,0,3,2:T(4,128)(2,1)}, u32[]{:S(2)}, u32[]{:S(2)}) collective-permute-start(bf16[2,4,1,8,256]{4,1,0,3,2:T(4,128)(2,1)} %get-tuple-element.23), channel_id=1, source_target_pairs={{2,0},{4,2},{6,4},{8,6},{10,8},{12,10},{14,12},{3,1},{5,3},{7,5},{... | collective-permute-start | bytes 98312 | tf_op jit(solution)/shard_map/ppermute | solution.py:17
  3.8 13.7 %collective-permute-start.1 = (bf16[2,4,1,8,256]{4,1,0,3,2:T(4,128)(2,1)}, bf16[2,4,1,8,256]{4,1,0,3,2:T(4,128)(2,1)}, u32[]{:S(2)}, u32[]{:S(2)}) collective-permute-start(bf16[2,4,1,8,256]{4,1,0,3,2:T(4,128)(2,1)} %get-tuple-element.24), channel_id=1, source_target_pairs={{0,2},{2,4},{4,6},{6,8},{8,10},{10,12},{12,14},{1,3},{3,5},{5,7},{... | collective-permute-start | bytes 98312 | tf_op jit(solution)/shard_map/ppermute | solution.py:14
  10.9 1.5 copy-start.6
  11.8 2.7 %copy-start.7 = (bf16[32,16,3,3,3]{0,1,4,3,2:T(8,128)(2,1)S(1)}, bf16[32,16,3,3,3]{0,1,4,3,2:T(8,128)(2,1)}, u32[]{:S(2)}) copy-start(bf16[32,16,3,3,3]{0,1,4,3,2:T(8,128)(2,1)} %param.9) | copy-start | bytes 82948
  13.2 11.2 %collective-permute-start = (bf16[1,32,1,8,128]{4,1,3,2,0:T(8,128)(2,1)S(1)}, bf16[1,32,1,8,128]{4,1,3,2,0:T(8,128)(2,1)S(1)}, u32[]{:S(2)}, u32[]{:S(2)}) collective-permute-start(bf16[1,32,1,8,128]{4,1,3,2,0:T(8,128)(2,1)S(1)} %slice.415), channel_id=1, source_target_pairs={{2,0},{4,2},{6,4},{8,6},{10,8},{12,10},{14,12},{3,1},{5,3},{7,5},{... | collective-permute-start | bytes 196616 | tf_op jit(solution)/shard_map/ppermute | solution.py:25
  20.2 4.9 %copy-start.2 = (bf16[2,4,10,8,256]{4,1,0,3,2:T(4,128)(2,1)}, bf16[2,4,10,8,256]{4,1,0,3,2:T(4,128)(2,1)S(1)}, u32[]{:S(2)}) copy-start(bf16[2,4,10,8,256]{4,1,0,3,2:T(4,128)(2,1)S(1)} %constant_dynamic-update-slice_fusion.7) | copy-start | bytes 983044
  21.0 45.5 %collective-permute-start.3 = (bf16[2,4,10,1,256]{4,1,0,3,2:T(4,128)(2,1)}, bf16[2,4,10,1,256]{4,1,0,3,2:T(4,128)(2,1)}, u32[]{:S(2)}, u32[]{:S(2)}) collective-permute-start(bf16[2,4,10,1,256]{4,1,0,3,2:T(4,128)(2,1)} %get-tuple-element.21), channel_id=1, source_target_pairs={{0,1},{2,3},{4,5},{6,7},{8,9},{10,11},{12,13},{14,15},{16,17},{18,... | collective-permute-start | bytes 122888 | tf_op jit(solution)/shard_map/ppermute | solution.py:14
  23.0 43.5 %collective-permute-start.4 = (bf16[2,4,10,1,256]{4,1,0,3,2:T(4,128)(2,1)}, bf16[2,4,10,1,256]{4,1,0,3,2:T(4,128)(2,1)}, u32[]{:S(2)}, u32[]{:S(2)}) collective-permute-start(bf16[2,4,10,1,256]{4,1,0,3,2:T(4,128)(2,1)} %get-tuple-element.22), channel_id=1, source_target_pairs={{1,0},{3,2},{5,4},{7,6},{9,8},{11,10},{13,12},{15,14},{17,16},{19,... | collective-permute-start | bytes 122888 | tf_op jit(solution)/shard_map/ppermute | solution.py:17
  24.8 0.9 copy-start.12
  24.8 0.9 copy-start.13
  24.9 1.1 copy-start.10
  24.9 1.1 copy-start.11
  25.1 1.2 copy-start.8
  25.2 1.2 copy-start.9
  25.2 1.2 copy-start.24
  25.2 1.2 copy-start.25
  26.0 0.7 copy-start.22
  26.1 0.7 copy-start.23
  26.4 0.7 copy-start.18
  26.4 0.7 copy-start.19
  26.4 0.7 copy-start.20
  26.4 0.7 copy-start.21
  26.8 0.7 copy-start.14
  26.8 0.7 copy-start.15
  26.8 0.7 copy-start.16
  49.4 5.9 %copy-start = (bf16[2,16,8,8,256]{4,3,2,1,0:T(8,128)(2,1)S(1)}, bf16[2,16,8,8,256]{4,3,2,1,0:T(8,128)(2,1)}, u32[]{:S(2)}) copy-start(bf16[2,16,8,8,256]{4,3,2,1,0:T(8,128)(2,1)} %param.6) | copy-start | bytes 3145732
  56.8 9.7 %copy-start.3 = (bf16[2,4,10,8,256]{4,1,0,3,2:T(4,128)(2,1)S(1)}, bf16[2,4,10,8,256]{4,1,0,3,2:T(4,128)(2,1)}, u32[]{:S(2)}) copy-start(bf16[2,4,10,8,256]{4,1,0,3,2:T(4,128)(2,1)} %copy-done.2) | copy-start | bytes 983044
  61.6 35.3 %collective-permute-start.5 = (bf16[1,16,1,16,256]{4,3,2,1,0:T(8,128)(2,1)S(1)}, bf16[1,16,1,16,256]{4,3,2,1,0:T(8,128)(2,1)S(1)}, u32[]{:S(2)}, u32[]{:S(2)}) collective-permute-start(bf16[1,16,1,16,256]{4,3,2,1,0:T(8,128)(2,1)S(1)} %slice.448), channel_id=1, source_target_pairs={{0,2},{2,4},{4,6},{6,8},{8,10},{10,12},{12,14},{1,3},{3,5},{5,7},{... | collective-permute-start | bytes 393224 | tf_op jit(solution)/shard_map/ppermute | solution.py:25
  70.3 1.7 copy-start.5
  80.1 1.7 copy-start.1
  164.7 2.2 copy-start.26
  (1 other events, 0.7 us)
where the time goes:
time: 233 us; the launch traced here: 231 us
  local copies, waits for them, and re-layouts  95.9 us (41%)
  blocking collectives  74.3 us (32%)
  matrix products  37.7 us (16%)
  starting transfers between devices  16.9 us (7%)
  other arithmetic  4.49 us (2%)
    psum x1, blocking collectives, on_device(): lax.psum((first_kernel, first_bias, deep_kernel, deep_bias), ('depth', 'h...  63.7 us
    reshape x2, local copies, waits for them, and re-layouts, deep_weight_grad(): grown.reshape(samples, chans, coarse_depth + 1, 2, coarse_height + 1, 2,...  46.6 us
    dot_general x27, matrix products, first_weight_grad(): jnp.einsum('sodhw,sidhw->oi', first_grad, view, preferred_element_type=jn...  29 us
    convert_element_type x2, local copies, waits for them, and re-layouts, transpose_conv(): return woven.astype(jnp.bfloat16)  21.2 us
    pad x1, local copies, waits for them, and re-layouts, deep_weight_grad(): grown = jnp.pad(padded, ((0, 0), (0, 0), (0, 1), (0, 1), (0, 1)))  10.9 us
    unnamed x64, local copies, waits for them, and re-layouts  10.4 us
    ppermute x2, starting transfers between devices, padded_2(): lax.ppermute(lax.slice_in_dim(block, block.shape[dim] - width, None, axis...  8.18 us
    ppermute x2, starting transfers between devices, from_behind(): lax.ppermute(value, axis, [(source, source + steps) for source in range(l...  6.15 us
  transfers between devices with their start and end apart: 6, of which 0 were waited for; matrix products, arithmetic and copies ran while one was open for 29% of the time, Pallas kernels for 0%

commit v1 on v0

--- a/solution.py
+++ b/solution.py
@@ -178,7 +178,7 @@
     ).astype(jnp.bfloat16)
     first_kernel, first_bias = first_weight_grad(first_grad, framed)
     first_kernel, first_bias, deep_kernel, deep_bias = lax.psum(
-        (first_kernel, first_bias, deep_kernel, deep_bias), ("depth", "height")
+        lax.psum((first_kernel, first_bias, deep_kernel, deep_bias), "height"), "depth"
     )
     return (first_kernel, first_bias, deep_kernel, deep_bias)
 

time: 233 us -> 214 us (0.918)
  blocking collectives: 74.3 us -> 54.7 us
    psum x1 -> x2, blocking collectives: 63.7 us -> 44.1 us  [the longest x1 40 us: on_device(): lax.psum(lax.psum((first_kernel, first_bias, deep_kernel, deep_bias), 'he...]
  transfers between devices with their start and end apart: 6 -> 6, of which waited for: 0 -> 0; matrix products, arithmetic and copies ran while one was open for 29% -> 31% of each run, Pallas kernels for 0% -> 0%
where the time goes in v1:
time: 214 us; the launch traced here: 211 us
  local copies, waits for them, and re-layouts  95.9 us (45%)
  blocking collectives  54.7 us (26%)
  matrix products  37.7 us (18%)
  starting transfers between devices  16.9 us (8%)
  other arithmetic  4.49 us (2%)
    reshape x2, local copies, waits for them, and re-layouts, deep_weight_grad(): grown.reshape(samples, chans, coarse_depth + 1, 2, coarse_height + 1, 2,...  46.6 us
    psum x1, blocking collectives, on_device(): lax.psum(lax.psum((first_kernel, first_bias, deep_kernel, deep_bias), 'he...  40 us
    dot_general x27, matrix products, first_weight_grad(): jnp.einsum('sodhw,sidhw->oi', first_grad, view, preferred_element_type=jn...  29 us
    convert_element_type x2, local copies, waits for them, and re-layouts, transpose_conv(): return woven.astype(jnp.bfloat16)  21.2 us
    pad x1, local copies, waits for them, and re-layouts, deep_weight_grad(): grown = jnp.pad(padded, ((0, 0), (0, 0), (0, 1), (0, 1), (0, 1)))  10.9 us
    unnamed x64, local copies, waits for them, and re-layouts  10.4 us
    ppermute x2, starting transfers between devices, padded_2(): lax.ppermute(lax.slice_in_dim(block, block.shape[dim] - width, None, axis...  8.18 us
    ppermute x2, starting transfers between devices, from_behind(): lax.ppermute(value, axis, [(source, source + steps) for source in range(l...  6.15 us
  transfers between devices with their start and end apart: 6, of which 0 were waited for; matrix products, arithmetic and copies ran while one was open for 31% of the time, Pallas kernels for 0%

profile of v1, /device:TPU:0, one launch (start us, length us, event | category | flops | bytes accessed | tf_op | source)
XLA Modules:
  0.0 210.9 jit_solution(17524903641963530051)
XLA Ops:
  0.6 1.2 copy.92
  2.5 1.3 collective-permute-start.2
  3.8 6.1 %collective-permute-start.1 = (bf16[2,4,1,8,256]{4,1,0,3,2:T(4,128)(2,1)}, bf16[2,4,1,8,256]{4,1,0,3,2:T(4,128)(2,1)}, u32[]{:S(2)}, u32[]{:S(2)}) collective-permute-start(bf16[2,4,1,8,256]{4,1,0,3,2:T(4,128)(2,1)} %get-tuple-element.28), channel_id=1, source_target_pairs={{0,2},{2,4},{4,6},{6,8},{8,10},{10,12},{12,14},{1,3},{3,5},{5,7},{... | collective-permute-start | bytes 98312 | tf_op jit(solution)/shard_map/ppermute | solution.py:14
  10.9 0.9 broadcast_in_dim.23
  13.2 1.3 collective-permute-start
  18.2 1.2 constant_dynamic-update-slice_fusion.8
  21.0 2.1 collective-permute-start.3
  23.0 1.3 collective-permute-start.4
  28.2 14.4 %copy.88 = bf16[2,2,2,1,16,4,8,128]{4,2,7,1,6,0,5,3:T(2,128)(2,1)} copy(bf16[2,2,2,1,16,4,8,128]{7,4,6,5,2,1,0,3:T(8,128)(2,1)S(1)} %bitcast.783) | data formatting | bytes 2097152 | tf_op jit(solution)/shard_map/convert_element_type | solution.py:129
  42.6 6.9 %copy.89 = bf16[1,16,8,16,256]{4,2,1,0,3:T(8,128)(2,1)S(1)} copy(bf16[1,16,8,16,256]{1,4,3,2,0:T(8,128)(2,1)} %bitcast.752) | data formatting | bytes 2097152 | tf_op jit(solution)/shard_map/convert_element_type | solution.py:129
  49.4 5.9 %all_to_all.27 = bf16[1,16,8,16,256]{4,2,1,0,3:T(8,128)(2,1)S(1)} all-to-all(bf16[1,16,8,16,256]{4,2,1,0,3:T(8,128)(2,1)S(1)} %copy.89), channel_id=1, replica_groups=mesh['groups'=2,'depth'=8,'height'=2] {'height'}, dimensions={3} | all-to-all | bytes 2097152 | tf_op jit(solution)/shard_map/all_to_all | solution.py:174
  55.4 1.3 convert_reduce_fusion
  56.8 4.7 %all_to_all.28 = bf16[2,16,8,8,256]{4,3,2,1,0:T(8,128)(2,1)S(1)} all-to-all(bf16[2,16,8,8,256]{4,3,2,1,0:T(8,128)(2,1)S(1)} %copy.125), channel_id=1, replica_groups=mesh['groups'=2,'depth'=8,'height'=2] {'height'}, dimensions={0} | all-to-all | bytes 2097152 | tf_op jit(solution)/shard_map/all_to_all | solution.py:164
  61.7 4.9 %collective-permute-start.5 = (bf16[1,16,1,16,256]{4,3,2,1,0:T(8,128)(2,1)S(1)}, bf16[1,16,1,16,256]{4,3,2,1,0:T(8,128)(2,1)S(1)}, u32[]{:S(2)}, u32[]{:S(2)}) collective-permute-start(bf16[1,16,1,16,256]{4,3,2,1,0:T(8,128)(2,1)S(1)} %slice.448), channel_id=1, source_target_pairs={{0,2},{2,4},{4,6},{6,8},{8,10},{10,12},{12,14},{1,3},{3,5},{5,7},{... | collective-permute-start | bytes 393224 | tf_op jit(solution)/shard_map/ppermute | solution.py:25
  66.6 1.4 select_maximum_fusion
  68.7 1.6 fusion.81
  70.3 0.9 fusion.80
  72.0 1.6 fusion.78
  75.3 1.6 fusion.75
  76.9 0.9 fusion.74
  78.6 1.6 fusion.72
  81.9 0.9 fusion.69
  84.4 1.8 fusion.66
  87.9 1.6 fusion.63
  91.2 1.6 fusion.60
  94.5 1.6 fusion.57
  97.1 6.5 %copy.193 = bf16[1,16,9,16,256]{1,4,3,2,0:T(8,128)(2,1)} copy(bf16[1,16,9,16,256]{4,3,2,1,0:T(8,128)(2,1)S(1)} %pad_maximum_fusion.4) | data formatting | bytes 2359296
  103.5 10.9 %pad.82 = bf16[1,16,10,18,258]{1,4,3,2,0:T(8,128)(2,1)} pad(bf16[1,16,9,16,256]{1,4,3,2,0:T(8,128)(2,1)} %copy.193, bf16[]{:T(256)} %constant.3.clone.1), padding=0_0x0_0x0_1x1_1x1_1 | pad | bytes 2665730 | tf_op jit(solution)/shard_map/jit(_pad)/pad | solution.py:59
  114.5 24.0 %reshape.237 = bf16[1,16,5,2,9,2,129,2]{1,7,6,5,4,3,2,0:T(2,128)(2,1)} reshape(bf16[1,16,10,18,258]{1,4,3,2,0:T(8,128)(2,1)} %pad.82) | data formatting | bytes 2972160 | tf_op jit(solution)/shard_map/reshape | solution.py:60
  138.5 22.6 %copy.128 = bf16[1,16,5,2,9,2,129,2]{6,1,4,2,7,5,3,0:T(8,128)(2,1)S(1)} copy(bf16[1,16,5,2,9,2,129,2]{1,7,6,5,4,3,2,0:T(2,128)(2,1)} %reshape.237) | data formatting | bytes 2972160 | tf_op jit(solution)/shard_map/reshape | solution.py:60
  166.9 4.0 %all-reduce.5 = (f32[16,4,3,3,3]{0,1,4,3,2:T(4,128)S(1)}, f32[16]{0:T(128)S(1)}, f32[32,16,3,3,3]{0,1,4,3,2:T(8,128)S(1)}, f32[32]{0:T(128)S(1)}) all-reduce(f32[16,4,3,3,3]{0,1,4,3,2:T(4,128)S(1)} %bitcast.786, f32[16]{0:T(128)S(1)} %get-tuple-element.14, ...), channel_id=1, replica_groups=mesh['groups'=2,'depth'=8,'height'=2] {'height'}, use_global_device_ids=true, to_apply=%region_0.1 | all-reduce | flops 15600 | bytes 124800 | tf_op jit(solution)/shard_map/psum | solution.py:181
  170.9 40.0 %all-reduce.4 = (f32[16,4,3,3,3]{0,1,4,3,2:T(4,128)}, f32[16]{0:T(128)}, f32[32,16,3,3,3]{0,1,4,3,2:T(8,128)}, f32[32]{0:T(128)}) all-reduce(f32[16,4,3,3,3]{0,1,4,3,2:T(4,128)S(1)} %get-tuple-element.8, f32[16]{0:T(128)S(1)} %get-tuple-element.9, ...), channel_id=1, replica_groups=mesh['groups'=2,'depth'=8,'height'=2] {'depth'}, use_global_device_ids=true, to_apply=%region_1.2 | all-reduce | flops 15600 | bytes 124800 | tf_op jit(solution)/shard_map/psum | solution.py:180
  (136 shorter events, 31.3 us)
Async XLA Ops:
  1.8 8.1 %copy-start.4 = (bf16[2,4,8,8,256]{4,1,0,3,2:T(4,128)(2,1)}, bf16[2,4,8,8,256]{4,1,0,3,2:T(4,128)(2,1)S(1)}, u32[]{:S(2)}) copy-start(bf16[2,4,8,8,256]{4,1,0,3,2:T(4,128)(2,1)S(1)} %copy.92) | copy-start | bytes 786436
  2.5 16.9 %collective-permute-start.2 = (bf16[2,4,1,8,256]{4,1,0,3,2:T(4,128)(2,1)}, bf16[2,4,1,8,256]{4,1,0,3,2:T(4,128)(2,1)}, u32[]{:S(2)}, u32[]{:S(2)}) collective-permute-start(bf16[2,4,1,8,256]{4,1,0,3,2:T(4,128)(2,1)} %get-tuple-element.27), channel_id=1, source_target_pairs={{2,0},{4,2},{6,4},{8,6},{10,8},{12,10},{14,12},{3,1},{5,3},{7,5},{... | collective-permute-start | bytes 98312 | tf_op jit(solution)/shard_map/ppermute | solution.py:17
  3.8 13.7 %collective-permute-start.1 = (bf16[2,4,1,8,256]{4,1,0,3,2:T(4,128)(2,1)}, bf16[2,4,1,8,256]{4,1,0,3,2:T(4,128)(2,1)}, u32[]{:S(2)}, u32[]{:S(2)}) collective-permute-start(bf16[2,4,1,8,256]{4,1,0,3,2:T(4,128)(2,1)} %get-tuple-element.28), channel_id=1, source_target_pairs={{0,2},{2,4},{4,6},{6,8},{8,10},{10,12},{12,14},{1,3},{3,5},{5,7},{... | collective-permute-start | bytes 98312 | tf_op jit(solution)/shard_map/ppermute | solution.py:14
  10.9 1.5 copy-start.6
  11.8 2.7 %copy-start.7 = (bf16[32,16,3,3,3]{0,1,4,3,2:T(8,128)(2,1)S(1)}, bf16[32,16,3,3,3]{0,1,4,3,2:T(8,128)(2,1)}, u32[]{:S(2)}) copy-start(bf16[32,16,3,3,3]{0,1,4,3,2:T(8,128)(2,1)} %param.9) | copy-start | bytes 82948
  13.2 11.2 %collective-permute-start = (bf16[1,32,1,8,128]{4,1,3,2,0:T(8,128)(2,1)S(1)}, bf16[1,32,1,8,128]{4,1,3,2,0:T(8,128)(2,1)S(1)}, u32[]{:S(2)}, u32[]{:S(2)}) collective-permute-start(bf16[1,32,1,8,128]{4,1,3,2,0:T(8,128)(2,1)S(1)} %slice.415), channel_id=1, source_target_pairs={{2,0},{4,2},{6,4},{8,6},{10,8},{12,10},{14,12},{3,1},{5,3},{7,5},{... | collective-permute-start | bytes 196616 | tf_op jit(solution)/shard_map/ppermute | solution.py:25
  20.2 4.9 %copy-start.2 = (bf16[2,4,10,8,256]{4,1,0,3,2:T(4,128)(2,1)}, bf16[2,4,10,8,256]{4,1,0,3,2:T(4,128)(2,1)S(1)}, u32[]{:S(2)}) copy-start(bf16[2,4,10,8,256]{4,1,0,3,2:T(4,128)(2,1)S(1)} %constant_dynamic-update-slice_fusion.7) | copy-start | bytes 983044
  21.0 45.6 %collective-permute-start.3 = (bf16[2,4,10,1,256]{4,1,0,3,2:T(4,128)(2,1)}, bf16[2,4,10,1,256]{4,1,0,3,2:T(4,128)(2,1)}, u32[]{:S(2)}, u32[]{:S(2)}) collective-permute-start(bf16[2,4,10,1,256]{4,1,0,3,2:T(4,128)(2,1)} %get-tuple-element.25), channel_id=1, source_target_pairs={{0,1},{2,3},{4,5},{6,7},{8,9},{10,11},{12,13},{14,15},{16,17},{18,... | collective-permute-start | bytes 122888 | tf_op jit(solution)/shard_map/ppermute | solution.py:14
  23.0 43.5 %collective-permute-start.4 = (bf16[2,4,10,1,256]{4,1,0,3,2:T(4,128)(2,1)}, bf16[2,4,10,1,256]{4,1,0,3,2:T(4,128)(2,1)}, u32[]{:S(2)}, u32[]{:S(2)}) collective-permute-start(bf16[2,4,10,1,256]{4,1,0,3,2:T(4,128)(2,1)} %get-tuple-element.26), channel_id=1, source_target_pairs={{1,0},{3,2},{5,4},{7,6},{9,8},{11,10},{13,12},{15,14},{17,16},{19,... | collective-permute-start | bytes 122888 | tf_op jit(solution)/shard_map/ppermute | solution.py:17
  24.8 0.9 copy-start.12
  24.8 0.9 copy-start.13
  24.9 1.1 copy-start.10
  24.9 1.1 copy-start.11
  25.1 1.2 copy-start.8
  25.1 1.2 copy-start.9
  25.2 1.2 copy-start.24
  25.2 1.2 copy-start.25
  26.0 0.7 copy-start.22
  26.0 0.7 copy-start.23
  26.4 0.7 copy-start.18
  26.4 0.7 copy-start.19
  26.4 0.7 copy-start.20
  26.4 0.7 copy-start.21
  26.7 0.7 copy-start.14
  26.8 0.7 copy-start.15
  26.8 0.7 copy-start.16
  49.4 5.9 %copy-start = (bf16[2,16,8,8,256]{4,3,2,1,0:T(8,128)(2,1)S(1)}, bf16[2,16,8,8,256]{4,3,2,1,0:T(8,128)(2,1)}, u32[]{:S(2)}) copy-start(bf16[2,16,8,8,256]{4,3,2,1,0:T(8,128)(2,1)} %param.6) | copy-start | bytes 3145732
  56.8 9.7 %copy-start.3 = (bf16[2,4,10,8,256]{4,1,0,3,2:T(4,128)(2,1)S(1)}, bf16[2,4,10,8,256]{4,1,0,3,2:T(4,128)(2,1)}, u32[]{:S(2)}) copy-start(bf16[2,4,10,8,256]{4,1,0,3,2:T(4,128)(2,1)} %copy-done.2) | copy-start | bytes 983044
  61.7 35.3 %collective-permute-start.5 = (bf16[1,16,1,16,256]{4,3,2,1,0:T(8,128)(2,1)S(1)}, bf16[1,16,1,16,256]{4,3,2,1,0:T(8,128)(2,1)S(1)}, u32[]{:S(2)}, u32[]{:S(2)}) collective-permute-start(bf16[1,16,1,16,256]{4,3,2,1,0:T(8,128)(2,1)S(1)} %slice.448), channel_id=1, source_target_pairs={{0,2},{2,4},{4,6},{6,8},{8,10},{10,12},{12,14},{1,3},{3,5},{5,7},{... | collective-permute-start | bytes 393224 | tf_op jit(solution)/shard_map/ppermute | solution.py:25
  70.3 1.7 copy-start.5
  80.2 1.7 copy-start.1
  164.7 2.2 %copy-start.26 = (f32[32]{0:T(128)S(1)}, f32[32]{0:T(128)}, u32[]{:S(2)}) copy-start(f32[32]{0:T(128)} %get-tuple-element.12) | copy-start | bytes 388
  (1 other events, 0.7 us)
